TPU v7x, 32 devices: a whole 2x2x4 slice. The times are simulated.
32 devices in a mesh: nest: 2 (over core), rows: 8 (over z, x), sub: 2 (over y).
Axes of the slice: x: 2, y: 2, z: 4, core: 2. Of those that a mesh axis runs over, the one named last changes fastest.
Arguments:
- elevation: float32 [2, 1024, 1024], P('nest', ('rows', 'sub')), may hold values from -6 to 6
- momentum_x: float32 [2, 1024, 1024], P('nest', ('rows', 'sub')), may hold values from -6 to 6
- momentum_y: float32 [2, 1024, 1024], P('nest', ('rows', 'sub')), may hold values from -6 to 6
- depth: float32 [2, 1024, 1024], P('nest', ('rows', 'sub')), may hold values from 0.2 to 1
- wet_mask: int32 [2, 1024, 1024], P('nest', ('rows', 'sub')), may hold values 0 or 1
- inverse_x: float32 [2, 8, 128, 128], P('nest'), may hold values from -1 to 2, as said below
- inverse_y: float32 [2, 8, 128, 128], P('nest'), may hold values from -1 to 2, as said below
- nest_map: int32 [2, 2, 1024], replicated, may hold values from 0 to 1023, as said below
Outputs:
- elevation_out: float32 [2, 1024, 1024], P('nest', ('rows', 'sub'))
- momentum_x_out: float32 [2, 1024, 1024], P('nest', ('rows', 'sub'))
- momentum_y_out: float32 [2, 1024, 1024], P('nest', ('rows', 'sub'))
Inputs may be any that keep to these rules, and one draw needn't show every extreme that they name: nest_map[b, 0, j] is the regional row and nest_map[b, 1, j] the regional column for cell j of the near-field's first (b = 0) or last (b = 1) row; the first row is driven by regional row 0 and the last by regional row 1023, and the column is c0 + j // 2 for one offset c0 shared by both rows, with every column below 1024. `inverse_x`: dense blocks, one for each line block of a section. `inverse_y`: dense blocks, one for each line block of a section.
All inputs are finite; a program needn't handle non-finite values. No bound on the sum of `wet_mask` on one device may be relied on, other than what follows from the above.
Results may differ from a plain program's by a relative error of at most 0.00013.
Values sent between devices are 32-bit elements; how exact they have to be, the bound alone decides.
No kernel may reach another device: no remote copies, remote signals or barrier semaphores. Data moves between devices by JAX's collectives and lax.ppermute only.
A program may use at most 64 MiB of HBM per device.

v0:
```python
import jax
import jax.numpy as jnp
from jax import lax
from jax.sharding import PartitionSpec as P

STEPS = 2
step_ratio = 0.5
dispersion = 0.5
nest_blend = 0.5


def from_behind(value, axis, steps):
    count = lax.axis_size(axis)
    leading, last = (max(0, -steps), min(count, count - steps))
    return lax.ppermute(value, axis, [(source, source + steps) for source in range(leading, last)])


def redistribute(blocks):
    return lax.all_to_all(blocks, ("rows", "sub"), split_axis=0, concat_axis=0, tiled=True)


def to_lines(field):
    rows_here, width = field.shape
    count = lax.axis_size(("rows", "sub"))
    blocks = field.reshape(rows_here, count, width // count).transpose(1, 0, 2)
    moved = redistribute(blocks)
    return moved.reshape(count * rows_here, width // count).T


def from_lines(lines):
    line_width, total_rows = lines.shape
    count = lax.axis_size(("rows", "sub"))
    rows_here = total_rows // count
    blocks = lines.T.reshape(count, rows_here, line_width)
    moved = redistribute(blocks)
    return moved.transpose(1, 0, 2).reshape(rows_here, count * line_width)


def operate_last(field, coef):
    right = jnp.pad(field[:, 1:], ((0, 0), (0, 1)))
    left = jnp.pad(field[:, :-1], ((0, 0), (1, 0)))
    coef_left = jnp.pad(coef[:, :-1], ((0, 0), (1, 0)))
    return field + coef * (field - right) + coef_left * (field - left)


def apply_blocks(field, tables):
    leading, length = field.shape
    group = tables.shape[-1]
    split = field.reshape(leading, length // group, group)
    result = jnp.einsum(
        "kij,rkj->rki",
        tables,
        split,
        precision=lax.Precision.HIGHEST,
        preferred_element_type=jnp.float32,
    )
    return result.reshape(leading, length)


def on_device(elevation, momentum_x, momentum_y, depth, wet_mask, inverse_x, inverse_y, nest_map):
    height = elevation[0]
    flow_x = momentum_x[0]
    flow_y = momentum_y[0]
    depth_here = depth[0]
    wetness = wet_mask[0].astype(jnp.float32)
    rows_here, width = height.shape
    total_rows = lax.axis_size(("rows", "sub")) * rows_here
    tables_x = inverse_x[0]
    tables_y = inverse_y[0]
    start = lax.axis_index(("rows", "sub")) * rows_here
    regional = lax.axis_index("nest") == 0
    nearfield = lax.axis_index("nest") == 1
    global_rows = start + lax.iota(jnp.int32, rows_here)
    top_row = jnp.logical_and(nearfield, global_rows == 0)[:, None]
    bottom_row = jnp.logical_and(nearfield, global_rows == total_rows - 1)[:, None]
    face_x = wetness[:, :-1] * wetness[:, 1:] * (0.5 * (depth_here[:, :-1] + depth_here[:, 1:]))
    face_x = jnp.pad(face_x, ((0, 0), (0, 1)))
    coef_x = dispersion * face_x * face_x
    face_y = jnp.zeros_like(height)
    coef_y = jnp.zeros_like(height)
    coef_lines = jnp.zeros_like(height)
    for step in range(STEPS):
        below = from_behind(jnp.stack([height[0], depth_here[0], wetness[0]]), ("rows", "sub"), -1)
        if step == 0:
            depth_next = jnp.concatenate([depth_here[1:], below[1:2]], 0)
            wet_next = jnp.concatenate([wetness[1:], below[2:3]], 0)
            face_y = wetness * wet_next * (0.5 * (depth_here + depth_next))
            coef_y = dispersion * face_y * face_y
            coef_lines = to_lines(coef_y)
        south = jnp.concatenate([height[1:], below[0:1]], 0)
        east = jnp.pad(height[:, 1:], ((0, 0), (0, 1)))
        push_x = flow_x + step_ratio * face_x * (east - height)
        push_y = flow_y + step_ratio * face_y * (south - height)
        first_x = apply_blocks(push_x, tables_x)
        flow_x = first_x + apply_blocks(push_x - operate_last(first_x, coef_x), tables_x)
        lines = to_lines(push_y)
        first_y = apply_blocks(lines, tables_y)
        flow_y = from_lines(
            first_y + apply_blocks(lines - operate_last(first_y, coef_lines), tables_y)
        )
        flux_x = face_x * flow_x
        flux_y = face_y * flow_y
        west = jnp.pad(flux_x[:, :-1], ((0, 0), (1, 0)))
        above = from_behind(flux_y[-1:], ("rows", "sub"), 1)
        north = jnp.concatenate([above, flux_y[:-1]], 0)
        height = height + step_ratio * (flux_x - west + flux_y - north)
        local_rows = nest_map[:, 0, :] - start
        owned = jnp.logical_and(jnp.logical_and(local_rows >= 0, local_rows < rows_here), regional)
        picked = height[jnp.clip(local_rows, 0, rows_here - 1), nest_map[:, 1, :]]
        packet = lax.psum(jnp.where(owned, picked, 0.0), ("nest", "rows", "sub"))
        blended_top = nest_blend * height + (1.0 - nest_blend) * packet[0][None, :]
        blended_bottom = nest_blend * height + (1.0 - nest_blend) * packet[1][None, :]
        height = jnp.where(top_row, blended_top, jnp.where(bottom_row, blended_bottom, height))
    return (height[None], flow_x[None], flow_y[None])


def solution(mesh):
    in_specs = (
        P("nest", ("rows", "sub"), None),
        P("nest", ("rows", "sub"), None),
        P("nest", ("rows", "sub"), None),
        P("nest", ("rows", "sub"), None),
        P("nest", ("rows", "sub"), None),
        P("nest", None, None, None),
        P("nest", None, None, None),
        P(),
    )
    out_specs = (
        P("nest", ("rows", "sub"), None),
        P("nest", ("rows", "sub"), None),
        P("nest", ("rows", "sub"), None),
    )
    return jax.shard_map(
        on_device, mesh=mesh, in_specs=in_specs, out_specs=out_specs, check_vma=False
    )
```

profile of v0, /device:TPU:0, one launch (start us, length us, event | category | flops | bytes accessed | tf_op | source)
XLA Modules:
  0.0 247.4 jit_solution(11802230985280122733)
XLA Ops:
  0.7 1.1 convert_bitcast_fusion
  1.8 1.3 collective-permute-start
  3.1 0.9 slice_bitcast_fusion.3
  4.4 0.9 squeeze.34
  5.5 1.0 concatenate.45
  6.5 0.9 concatenate.48
  7.4 0.9 concatenate.51
  8.5 0.8 slice.195
  9.6 1.6 fusion.2
  11.5 1.0 reshape.253
  12.6 9.6 %all-to-all-start = ((f32[16,1,4096]{2,1,0:T(1,128)}), f32[16,1,4096]{2,1,0:T(1,128)S(1)}, u32[]{:S(2)}, u32[]{:S(2)}) async-start(f32[16,1,4096]{2,1,0:T(1,128)} %reshape.253), calls=%async_computation | async-start | bytes 524288 | tf_op jit(solution)/shard_map/all_to_all | solution.py:19
  23.0 1.1 convolution_bitcast_fusion.5
  24.1 0.9 fusion.58
  25.2 1.0 reshape.255
  26.2 5.5 %all-to-all-done = f32[16,1,4096]{2,1,0:T(1,128)S(1)} async-done(((f32[16,1,4096]{2,1,0:T(1,128)}), f32[16,1,4096]{2,1,0:T(1,128)S(1)}, u32[]{:S(2)}, u32[]{:S(2)}) %all-to-all-start) | async-done | bytes 262176 | tf_op jit(solution)/shard_map/all_to_all | solution.py:19
  31.8 4.2 %all-to-all-start.1 = ((f32[16,1,4096]{2,1,0:T(1,128)}), f32[16,1,4096]{2,1,0:T(1,128)}, u32[]{:S(2)}, u32[]{:S(2)}) async-start(f32[16,1,4096]{2,1,0:T(1,128)} %reshape.255), calls=%async_computation.1 | async-start | bytes 524288 | tf_op jit(solution)/shard_map/all_to_all | solution.py:19
  36.5 1.3 reduce.12
  37.8 1.0 reshape.254
  38.8 1.3 copy.88
  40.1 1.1 convolution_bitcast_fusion.3
  41.3 0.8 fusion.59
  42.0 2.4 all-to-all-done.1
  44.4 2.2 reduce.13
  46.7 1.0 reshape.256
  47.7 1.2 copy.89
  48.9 2.2 convolution_bitcast_fusion.2
  51.2 1.0 copy.191
  52.2 2.1 reshape.257
  54.2 4.6 %all-to-all-start.2 = ((f32[16,1,4096]{2,1,0:T(1,128)}), f32[16,1,4096]{2,1,0:T(1,128)S(1)}, u32[]{:S(2)}, u32[]{:S(2)}) async-start(f32[16,1,4096]{2,1,0:T(1,128)} %reshape.257), calls=%async_computation.2 | async-start | bytes 524288 | tf_op jit(solution)/shard_map/all_to_all | solution.py:19
  58.8 2.2 convolution_bitcast_fusion.4
  61.8 5.5 %all-to-all-done.2 = f32[16,1,4096]{2,1,0:T(1,128)S(1)} async-done(((f32[16,1,4096]{2,1,0:T(1,128)}), f32[16,1,4096]{2,1,0:T(1,128)S(1)}, u32[]{:S(2)}, u32[]{:S(2)}) %all-to-all-start.2) | async-done | bytes 262176 | tf_op jit(solution)/shard_map/all_to_all | solution.py:19
  67.3 1.3 reduce.14
  68.5 1.0 reshape.258
  69.6 1.2 copy.90
  70.8 1.3 fusion.53
  72.1 3.4 %collective-permute-start.1 = (f32[1,1024]{1,0:T(1,128)S(1)}, f32[1,1024]{1,0:T(1,128)S(1)}, u32[]{:S(2)}, u32[]{:S(2)}) collective-permute-start(f32[1,1024]{1,0:T(1,128)S(1)} %slice.208), channel_id=1, source_target_pairs={{0,1},{1,2},{2,3},{3,4},{4,5},{5,6},{6,7},{7,8},{8,9},{9,10},{10,1... | collective-permute-start | bytes 12296 | tf_op jit(solution)/shard_map/ppermute | solution.py:15
  75.5 1.3 collective-permute-done.1
  76.9 16.6 %gather_fusion = f32[2048]{0:T(1024)S(1)} fusion(f32[64,1024]{1,0:T(8,128)S(1)} %fusion.41, s32[2048]{0:T(1024)S(1)} %bitcast.265), kind=kCustom, calls=%fused_computation | custom fusion | bytes 32768 | tf_op jit(solution)/shard_map/gather | solution.py:109
  93.6 41.4 %psum.14 = f32[2,1024]{1,0:T(2,128)S(1)} all-reduce(f32[2,1024]{1,0:T(2,128)S(1)} %bitcast_select_fusion.1), channel_id=1, replica_groups=mesh['nest'=2,'rows'=8,'sub'=2] {'nest','rows','sub'}, use_global_device_ids=true, to_apply=%region_0.1 | all-reduce | flops 2048 | bytes 16384 | tf_op jit(solution)/shard_map/psum | solution.py:110
  135.2 1.3 collective-permute-start.2
  136.7 4.4 %collective-permute-done.2 = f32[3,1024]{1,0:T(4,128)S(1)} collective-permute-done((f32[3,1024]{1,0:T(4,128)S(1)}, f32[3,1024]{1,0:T(4,128)S(1)}, u32[]{:S(2)}, u32[]{:S(2)}) %collective-permute-start.2) | collective-permute-done | bytes 12320 | tf_op jit(solution)/shard_map/ppermute | solution.py:15
  141.2 1.0 fusion.16
  142.1 2.0 copy.91
  144.2 2.1 reshape.259
  146.2 5.7 %all-to-all-start.3 = ((f32[16,1,4096]{2,1,0:T(1,128)}), f32[16,1,4096]{2,1,0:T(1,128)S(1)}, u32[]{:S(2)}, u32[]{:S(2)}) async-start(f32[16,1,4096]{2,1,0:T(1,128)} %reshape.259), calls=%async_computation.3 | async-start | bytes 524288 | tf_op jit(solution)/shard_map/all_to_all | solution.py:19
  151.9 1.1 fusion.11
  153.1 7.3 %all-to-all-done.3 = f32[16,1,4096]{2,1,0:T(1,128)S(1)} async-done(((f32[16,1,4096]{2,1,0:T(1,128)}), f32[16,1,4096]{2,1,0:T(1,128)S(1)}, u32[]{:S(2)}, u32[]{:S(2)}) %all-to-all-start.3) | async-done | bytes 262176 | tf_op jit(solution)/shard_map/all_to_all | solution.py:19
  160.4 1.3 reduce.15
  161.6 1.0 reshape.260
  162.6 2.1 copy.79
  164.8 1.2 reshape.217
  166.0 1.1 convolution_bitcast_fusion.1
  167.3 1.2 convolution_bitcast_fusion
  168.8 1.0 reshape.261
  169.8 3.5 %all-to-all-start.4 = ((f32[16,1,4096]{2,1,0:T(1,128)}), f32[16,1,4096]{2,1,0:T(1,128)S(1)}, u32[]{:S(2)}, u32[]{:S(2)}) async-start(f32[16,1,4096]{2,1,0:T(1,128)} %reshape.261), calls=%async_computation.4 | async-start | bytes 524288 | tf_op jit(solution)/shard_map/all_to_all | solution.py:19
  173.5 0.8 copy-done.5
  174.3 1.9 bitcast_add_fusion.4
  176.2 5.6 %all-to-all-done.4 = f32[16,1,4096]{2,1,0:T(1,128)S(1)} async-done(((f32[16,1,4096]{2,1,0:T(1,128)}), f32[16,1,4096]{2,1,0:T(1,128)S(1)}, u32[]{:S(2)}, u32[]{:S(2)}) %all-to-all-start.4) | async-done | bytes 262176 | tf_op jit(solution)/shard_map/all_to_all | solution.py:19
  181.9 1.3 reduce.16
  183.6 3.5 %collective-permute-start.3 = (f32[1,1024]{1,0:T(1,128)S(1)}, f32[1,1024]{1,0:T(1,128)S(1)}, u32[]{:S(2)}, u32[]{:S(2)}) collective-permute-start(f32[1,1024]{1,0:T(1,128)S(1)} %slice.221), channel_id=1, source_target_pairs={{0,1},{1,2},{2,3},{3,4},{4,5},{5,6},{6,7},{7,8},{8,9},{9,10},{10,1... | collective-permute-start | bytes 12296 | tf_op jit(solution)/shard_map/ppermute | solution.py:15
  188.1 0.9 copy.93
  189.2 16.6 %gather_fusion.1 = f32[2048]{0:T(1024)S(1)} fusion(f32[64,1024]{1,0:T(8,128)S(1)} %fusion.45, s32[2048]{0:T(1024)S(1)} %bitcast.266), kind=kCustom, calls=%fused_computation.1 | custom fusion | bytes 32768 | tf_op jit(solution)/shard_map/gather | solution.py:109
  205.9 40.7 %psum.15 = f32[2,1024]{1,0:T(2,128)S(1)} all-reduce(f32[2,1024]{1,0:T(2,128)S(1)} %bitcast_select_fusion), channel_id=1, replica_groups=mesh['nest'=2,'rows'=8,'sub'=2] {'nest','rows','sub'}, use_global_device_ids=true, to_apply=%region_1.2 | all-reduce | flops 2048 | bytes 16384 | tf_op jit(solution)/shard_map/psum | solution.py:110
  246.5 0.9 select_bitcast_fusion
  (85 shorter events, 6.6 us)
Async XLA Ops:
  0.6 22.3 %copy-start = (f32[1,8,128,128]{3,2,1,0:T(8,128)S(1)}, f32[1,8,128,128]{3,2,1,0:T(8,128)}, u32[]{:S(2)}) copy-start(f32[1,8,128,128]{3,2,1,0:T(8,128)} %param.13) | copy-start | bytes 1572868
  0.6 1.1 copy-start.3
  0.7 1.2 copy-start.2
  1.8 7.5 %collective-permute-start = (f32[3,1024]{1,0:T(4,128)S(1)}, f32[3,1024]{1,0:T(4,128)S(1)}, u32[]{:S(2)}, u32[]{:S(2)}) collective-permute-start(f32[3,1024]{1,0:T(4,128)S(1)} %pad_maximum_fusion.1), channel_id=1, source_target_pairs={{1,0},{2,1},{3,2},{4,3},{5,4},{6,5},{7,6},{8,7},{9,8},{10,9},{11,1... | collective-permute-start | bytes 36872 | tf_op jit(solution)/shard_map/ppermute | solution.py:15
  7.4 0.9 copy-start.12
  9.6 1.6 copy-start.9
  12.6 9.6 %copy-start.11 = (f32[64,1023]{1,0:T(8,128)S(1)}, f32[64,1023]{1,0:T(8,128)}, u32[]{:S(2)}) copy-start(f32[64,1023]{1,0:T(8,128)} %slice.195) | copy-start | bytes 785668
  12.6 9.6 %copy-start.13 = (f32[1,64,1024]{2,1,0:T(8,128)S(1)}, f32[1,64,1024]{2,1,0:T(8,128)}, u32[]{:S(2)}) copy-start(f32[1,64,1024]{2,1,0:T(8,128)} %param.9) | copy-start | bytes 786436
  12.6 19.2 %all-to-all-start = ((f32[16,1,4096]{2,1,0:T(1,128)}), f32[16,1,4096]{2,1,0:T(1,128)S(1)}, u32[]{:S(2)}, u32[]{:S(2)}) async-start(f32[16,1,4096]{2,1,0:T(1,128)} %reshape.253), calls=%async_computation | async-start | bytes 524288 | tf_op jit(solution)/shard_map/all_to_all | solution.py:19
  22.3 0.7 copy-start.6
  26.2 9.7 %copy-start.14 = (s32[2,2,1024]{2,1,0:T(2,128)S(1)}, s32[2,2,1024]{2,1,0:T(2,128)}, u32[]{:S(2)}) copy-start(s32[2,2,1024]{2,1,0:T(2,128)} %param.15) | copy-start | bytes 49156
  31.8 12.7 %all-to-all-start.1 = ((f32[16,1,4096]{2,1,0:T(1,128)}), f32[16,1,4096]{2,1,0:T(1,128)}, u32[]{:S(2)}, u32[]{:S(2)}) async-start(f32[16,1,4096]{2,1,0:T(1,128)} %reshape.255), calls=%async_computation.1 | async-start | bytes 524288 | tf_op jit(solution)/shard_map/all_to_all | solution.py:19
  38.8 1.3 copy-start.1
  54.2 4.6 %copy-start.7 = (f32[64,1024]{1,0:T(8,128)S(1)}, f32[64,1024]{1,0:T(8,128)}, u32[]{:S(2)}) copy-start(f32[64,1024]{1,0:T(8,128)} %copy-done.6) | copy-start | bytes 786436
  54.2 13.0 %all-to-all-start.2 = ((f32[16,1,4096]{2,1,0:T(1,128)}), f32[16,1,4096]{2,1,0:T(1,128)S(1)}, u32[]{:S(2)}, u32[]{:S(2)}) async-start(f32[16,1,4096]{2,1,0:T(1,128)} %reshape.257), calls=%async_computation.2 | async-start | bytes 524288 | tf_op jit(solution)/shard_map/all_to_all | solution.py:19
  70.8 6.0 %copy-start.8 = (f32[64,1024]{1,0:T(8,128)S(1)}, f32[64,1024]{1,0:T(8,128)}, u32[]{:S(2)}) copy-start(f32[64,1024]{1,0:T(8,128)} %pad_multiply_fusion) | copy-start | bytes 786436
  72.1 4.7 %collective-permute-start.1 = (f32[1,1024]{1,0:T(1,128)S(1)}, f32[1,1024]{1,0:T(1,128)S(1)}, u32[]{:S(2)}, u32[]{:S(2)}) collective-permute-start(f32[1,1024]{1,0:T(1,128)S(1)} %slice.208), channel_id=1, source_target_pairs={{0,1},{1,2},{2,3},{3,4},{4,5},{5,6},{6,7},{7,8},{8,9},{9,10},{10,1... | collective-permute-start | bytes 12296 | tf_op jit(solution)/shard_map/ppermute | solution.py:15
  135.2 5.9 %collective-permute-start.2 = (f32[3,1024]{1,0:T(4,128)S(1)}, f32[3,1024]{1,0:T(4,128)S(1)}, u32[]{:S(2)}, u32[]{:S(2)}) collective-permute-start(f32[3,1024]{1,0:T(4,128)S(1)} %pad_maximum_fusion), channel_id=1, source_target_pairs={{1,0},{2,1},{3,2},{4,3},{5,4},{6,5},{7,6},{8,7},{9,8},{10,9},{11,1... | collective-permute-start | bytes 36872 | tf_op jit(solution)/shard_map/ppermute | solution.py:15
  142.1 9.8 %copy-start.4 = (f32[64,1024]{1,0:T(8,128)}, f32[64,1024]{1,0:T(8,128)S(1)}, u32[]{:S(2)}) copy-start(f32[64,1024]{1,0:T(8,128)S(1)} %get-tuple-element.12) | copy-start | bytes 786436
  146.2 14.1 %all-to-all-start.3 = ((f32[16,1,4096]{2,1,0:T(1,128)}), f32[16,1,4096]{2,1,0:T(1,128)S(1)}, u32[]{:S(2)}, u32[]{:S(2)}) async-start(f32[16,1,4096]{2,1,0:T(1,128)} %reshape.259), calls=%async_computation.3 | async-start | bytes 524288 | tf_op jit(solution)/shard_map/all_to_all | solution.py:19
  169.8 12.0 %all-to-all-start.4 = ((f32[16,1,4096]{2,1,0:T(1,128)}), f32[16,1,4096]{2,1,0:T(1,128)S(1)}, u32[]{:S(2)}, u32[]{:S(2)}) async-start(f32[16,1,4096]{2,1,0:T(1,128)} %reshape.261), calls=%async_computation.4 | async-start | bytes 524288 | tf_op jit(solution)/shard_map/all_to_all | solution.py:19
  173.4 1.0 copy-start.5
  183.5 3.6 %copy-start.10 = (f32[8,64,128]{2,1,0:T(8,128)S(1)}, f32[8,64,128]{2,1,0:T(8,128)}, u32[]{:S(2)}) copy-start(f32[8,64,128]{2,1,0:T(8,128)} %get-tuple-element.35) | copy-start | bytes 786436
  183.6 5.4 %collective-permute-start.3 = (f32[1,1024]{1,0:T(1,128)S(1)}, f32[1,1024]{1,0:T(1,128)S(1)}, u32[]{:S(2)}, u32[]{:S(2)}) collective-permute-start(f32[1,1024]{1,0:T(1,128)S(1)} %slice.221), channel_id=1, source_target_pairs={{0,1},{1,2},{2,3},{3,4},{4,5},{5,6},{6,7},{7,8},{8,9},{9,10},{10,1... | collective-permute-start | bytes 12296 | tf_op jit(solution)/shard_map/ppermute | solution.py:15
where the time goes:
time: 249 us; the launch traced here: 247 us
  blocking collectives  82.1 us (33%)
  local copies, waits for them, and re-layouts  68.1 us (27%)
  starting transfers between devices  37 us (15%)
  waiting for transfers between devices  32.1 us (13%)
  other arithmetic  15.1 us (6%)
  matrix products  11.9 us (5%)
    psum x2, blocking collectives, on_device(): packet = lax.psum(jnp.where(owned, picked, 0.0), ('nest', 'rows', 'sub'))  82.1 us
    gather x4, local copies, waits for them, and re-layouts, on_device(): picked = height[jnp.clip(local_rows, 0, rows_here - 1), nest_map[:, 1, :]]  33.3 us
    all_to_all x5, starting transfers between devices, redistribute(): lax.all_to_all(blocks, ('rows', 'sub'), split_axis=0, concat_axis=0, tile...  27.5 us
    all_to_all x5, waiting for transfers between devices, redistribute(): lax.all_to_all(blocks, ('rows', 'sub'), split_axis=0, concat_axis=0, tile...  26.3 us
    unnamed x40, local copies, waits for them, and re-layouts  13.1 us
    dot_general x8, matrix products, apply_blocks(): jnp.einsum('kij,rkj->rki', tables, split, precision=lax.Precision.HIGHEST...  11.9 us
    ppermute x4, starting transfers between devices, from_behind(): lax.ppermute(value, axis, [(source, source + steps) for source in range(l...  9.45 us
    all_to_all x5, other arithmetic, redistribute(): lax.all_to_all(blocks, ('rows', 'sub'), split_axis=0, concat_axis=0, tile...  7.24 us
  transfers between devices with their start and end apart: 9, of which 7 were waited for; matrix products, arithmetic and copies ran while one was open for 10% of the time, Pallas kernels for 0%

commit v1 on v0

--- a/solution.py
+++ b/solution.py
@@ -107,7 +107,9 @@
         local_rows = nest_map[:, 0, :] - start
         owned = jnp.logical_and(jnp.logical_and(local_rows >= 0, local_rows < rows_here), regional)
         picked = height[jnp.clip(local_rows, 0, rows_here - 1), nest_map[:, 1, :]]
-        packet = lax.psum(jnp.where(owned, picked, 0.0), ("nest", "rows", "sub"))
+        own = jnp.where(owned, picked, 0.0)
+        parts = lax.all_gather(own, ("nest", "rows", "sub"), axis=0, tiled=False)
+        packet = parts.sum(axis=0)
         blended_top = nest_blend * height + (1.0 - nest_blend) * packet[0][None, :]
         blended_bottom = nest_blend * height + (1.0 - nest_blend) * packet[1][None, :]
         height = jnp.where(top_row, blended_top, jnp.where(bottom_row, blended_bottom, height))

time: 249 us -> 301 us (1.21)
  blocking collectives: 82.1 us -> 134 us
  local copies, waits for them, and re-layouts: 68.1 us -> 64.9 us
    all_gather x0 -> x2, blocking collectives: none -> 134 us  [on_device(): parts = lax.all_gather(own, ('nest', 'rows', 'sub'), axis=0, tiled=False)]
    psum x2 -> x0, blocking collectives: 82.1 us -> none  [on_device(): packet = lax.psum(jnp.where(owned, picked, 0.0), ('nest', 'rows', 'sub'))]
    unnamed x40 -> x39, local copies, waits for them, and re-layouts: 13.1 us -> 10.6 us
  transfers between devices with their start and end apart: 9 -> 9, of which waited for: 7 -> 7; matrix products, arithmetic and copies ran while one was open for 10% -> 8% of each run, Pallas kernels for 0% -> 0%
where the time goes in v1:
time: 301 us; the launch traced here: 298 us
  blocking collectives  134 us (45%)
  local copies, waits for them, and re-layouts  64.9 us (22%)
  starting transfers between devices  35.2 us (12%)
  waiting for transfers between devices  33.6 us (11%)
  other arithmetic  17.9 us (6%)
  matrix products  12 us (4%)
    all_gather x2, blocking collectives, on_device(): parts = lax.all_gather(own, ('nest', 'rows', 'sub'), axis=0, tiled=False)  134 us
    gather x4, local copies, waits for them, and re-layouts, on_device(): picked = height[jnp.clip(local_rows, 0, rows_here - 1), nest_map[:, 1, :]]  33.3 us
    all_to_all x5, waiting for transfers between devices, redistribute(): lax.all_to_all(blocks, ('rows', 'sub'), split_axis=0, concat_axis=0, tile...  28.2 us
    all_to_all x5, starting transfers between devices, redistribute(): lax.all_to_all(blocks, ('rows', 'sub'), split_axis=0, concat_axis=0, tile...  26.4 us
    dot_general x8, matrix products, apply_blocks(): jnp.einsum('kij,rkj->rki', tables, split, precision=lax.Precision.HIGHEST...  12 us
    unnamed x39, local copies, waits for them, and re-layouts  10.6 us
    ppermute x4, starting transfers between devices, from_behind(): lax.ppermute(value, axis, [(source, source + steps) for source in range(l...  8.75 us
    all_to_all x5, other arithmetic, redistribute(): lax.all_to_all(blocks, ('rows', 'sub'), split_axis=0, concat_axis=0, tile...  8.21 us
  transfers between devices with their start and end apart: 9, of which 7 were waited for; matrix products, arithmetic and copies ran while one was open for 8% of the time, Pallas kernels for 0%

profile of v1, /device:TPU:0, one launch (start us, length us, event | category | flops | bytes accessed | tf_op | source)
XLA Modules:
  0.0 298.4 jit_solution(8183487731271727504)
XLA Ops:
  0.7 1.1 convert_bitcast_fusion
  1.8 1.3 collective-permute-start
  3.1 0.9 slice_bitcast_fusion.3
  4.3 1.0 squeeze.34
  5.5 1.0 concatenate.45
  6.4 0.9 concatenate.48
  7.4 0.9 concatenate.51
  8.5 0.8 slice.195
  9.6 1.6 fusion.2
  11.5 1.0 reshape.295
  12.5 9.6 %all-to-all-start = ((f32[16,1,4096]{2,1,0:T(1,128)}), f32[16,1,4096]{2,1,0:T(1,128)}, u32[]{:S(2)}, u32[]{:S(2)}) async-start(f32[16,1,4096]{2,1,0:T(1,128)} %reshape.295), calls=%async_computation | async-start | bytes 524288 | tf_op jit(solution)/shard_map/all_to_all | solution.py:19
  22.3 1.1 convolution_bitcast_fusion.5
  23.5 0.9 fusion.59
  24.5 1.0 reshape.297
  25.5 6.3 %all-to-all-done = f32[16,1,4096]{2,1,0:T(1,128)} async-done(((f32[16,1,4096]{2,1,0:T(1,128)}), f32[16,1,4096]{2,1,0:T(1,128)}, u32[]{:S(2)}, u32[]{:S(2)}) %all-to-all-start) | async-done | bytes 262176 | tf_op jit(solution)/shard_map/all_to_all | solution.py:19
  31.8 4.2 %all-to-all-start.1 = ((f32[16,1,4096]{2,1,0:T(1,128)}), f32[16,1,4096]{2,1,0:T(1,128)}, u32[]{:S(2)}, u32[]{:S(2)}) async-start(f32[16,1,4096]{2,1,0:T(1,128)} %reshape.297), calls=%async_computation.1 | async-start | bytes 524288 | tf_op jit(solution)/shard_map/all_to_all | solution.py:19
  36.6 2.2 reduce.12
  38.9 1.0 reshape.296
  39.9 1.3 copy.90
  41.2 1.1 convolution_bitcast_fusion.3
  42.4 0.9 fusion.60
  43.2 1.3 all-to-all-done.1
  44.5 2.2 reduce.13
  46.7 1.0 reshape.298
  47.8 1.2 copy.91
  49.0 2.2 convolution_bitcast_fusion.2
  52.0 1.1 reshape.250
  53.1 1.0 copy.209
  54.0 2.1 reshape.299
  56.1 5.5 %all-to-all-start.2 = ((f32[16,1,4096]{2,1,0:T(1,128)}), f32[16,1,4096]{2,1,0:T(1,128)S(1)}, u32[]{:S(2)}, u32[]{:S(2)}) async-start(f32[16,1,4096]{2,1,0:T(1,128)} %reshape.299), calls=%async_computation.2 | async-start | bytes 524288 | tf_op jit(solution)/shard_map/all_to_all | solution.py:19
  61.6 2.2 convolution_bitcast_fusion.4
  64.6 5.4 %all-to-all-done.2 = f32[16,1,4096]{2,1,0:T(1,128)S(1)} async-done(((f32[16,1,4096]{2,1,0:T(1,128)}), f32[16,1,4096]{2,1,0:T(1,128)S(1)}, u32[]{:S(2)}, u32[]{:S(2)}) %all-to-all-start.2) | async-done | bytes 262176 | tf_op jit(solution)/shard_map/all_to_all | solution.py:19
  70.1 1.3 reduce.14
  71.8 1.2 fusion.54
  73.0 3.4 %collective-permute-start.1 = (f32[1,1024]{1,0:T(1,128)S(1)}, f32[1,1024]{1,0:T(1,128)S(1)}, u32[]{:S(2)}, u32[]{:S(2)}) collective-permute-start(f32[1,1024]{1,0:T(1,128)S(1)} %slice.208), channel_id=1, source_target_pairs={{0,1},{1,2},{2,3},{3,4},{4,5},{5,6},{6,7},{7,8},{8,9},{9,10},{10,1... | collective-permute-start | bytes 12296 | tf_op jit(solution)/shard_map/ppermute | solution.py:15
  76.4 1.3 collective-permute-done.1
  77.7 1.2 fusion.41
  78.9 16.6 %gather_fusion = f32[2048]{0:T(1024)S(1)} fusion(f32[64,1024]{1,0:T(8,128)S(1)} %fusion.41, s32[2048]{0:T(1024)S(1)} %bitcast.276), kind=kCustom, calls=%fused_computation | custom fusion | bytes 32768 | tf_op jit(solution)/shard_map/gather | solution.py:109
  95.6 67.2 %all_gather.8 = f32[32,2,1024]{2,1,0:T(2,128)S(1)} all-gather(f32[1,2,1024]{2,1,0:T(2,128)S(1)} %bitcast_select_fusion.1), channel_id=1, replica_groups=mesh['nest'=2,'rows'=8,'sub'=2] {'nest','rows','sub'}, dimensions={0}, use_global_device_ids=true | all-gather | bytes 270336 | tf_op jit(solution)/shard_map/all_gather | solution.py:111
  163.1 1.3 collective-permute-start.2
  164.5 4.2 %collective-permute-done.2 = f32[3,1024]{1,0:T(4,128)S(1)} collective-permute-done((f32[3,1024]{1,0:T(4,128)S(1)}, f32[3,1024]{1,0:T(4,128)S(1)}, u32[]{:S(2)}, u32[]{:S(2)}) %collective-permute-start.2) | collective-permute-done | bytes 12320 | tf_op jit(solution)/shard_map/ppermute | solution.py:15
  168.7 1.0 fusion.16
  169.7 1.2 copy.93
  170.9 1.0 reshape.301
  171.9 3.5 %all-to-all-start.3 = ((f32[16,1,4096]{2,1,0:T(1,128)}), f32[16,1,4096]{2,1,0:T(1,128)S(1)}, u32[]{:S(2)}, u32[]{:S(2)}) async-start(f32[16,1,4096]{2,1,0:T(1,128)} %reshape.301), calls=%async_computation.3 | async-start | bytes 524288 | tf_op jit(solution)/shard_map/all_to_all | solution.py:19
  175.5 1.1 fusion.11
  176.6 8.7 %all-to-all-done.3 = f32[16,1,4096]{2,1,0:T(1,128)S(1)} async-done(((f32[16,1,4096]{2,1,0:T(1,128)}), f32[16,1,4096]{2,1,0:T(1,128)S(1)}, u32[]{:S(2)}, u32[]{:S(2)}) %all-to-all-start.3) | async-done | bytes 262176 | tf_op jit(solution)/shard_map/all_to_all | solution.py:19
  185.4 1.3 reduce.15
  186.6 1.0 reshape.302
  187.6 2.1 copy.81
  189.8 1.2 reshape.257
  191.0 1.1 convolution_bitcast_fusion.1
  192.3 1.2 convolution_bitcast_fusion
  193.8 1.0 reshape.303
  194.9 3.5 %all-to-all-start.4 = ((f32[16,1,4096]{2,1,0:T(1,128)}), f32[16,1,4096]{2,1,0:T(1,128)S(1)}, u32[]{:S(2)}, u32[]{:S(2)}) async-start(f32[16,1,4096]{2,1,0:T(1,128)} %reshape.303), calls=%async_computation.4 | async-start | bytes 524288 | tf_op jit(solution)/shard_map/all_to_all | solution.py:19
  198.5 0.8 copy-done.7
  199.3 1.9 bitcast_add_fusion.4
  201.2 6.4 %all-to-all-done.4 = f32[16,1,4096]{2,1,0:T(1,128)S(1)} async-done(((f32[16,1,4096]{2,1,0:T(1,128)}), f32[16,1,4096]{2,1,0:T(1,128)S(1)}, u32[]{:S(2)}, u32[]{:S(2)}) %all-to-all-start.4) | async-done | bytes 262176 | tf_op jit(solution)/shard_map/all_to_all | solution.py:19
  207.6 1.3 reduce.16
  209.4 2.8 collective-permute-start.3
  213.1 0.9 copy.95
  214.2 16.6 %gather_fusion.1 = f32[2048]{0:T(1024)S(1)} fusion(f32[64,1024]{1,0:T(8,128)S(1)} %fusion.45, s32[2048]{0:T(1024)S(1)} %bitcast.277), kind=kCustom, calls=%fused_computation.1 | custom fusion | bytes 32768 | tf_op jit(solution)/shard_map/gather | solution.py:109
  230.9 66.4 %all_gather.9 = f32[32,2,1024]{2,1,0:T(2,128)S(1)} all-gather(f32[1,2,1024]{2,1,0:T(2,128)S(1)} %bitcast_select_fusion), channel_id=1, replica_groups=mesh['nest'=2,'rows'=8,'sub'=2] {'nest','rows','sub'}, dimensions={0}, use_global_device_ids=true | all-gather | bytes 270336 | tf_op jit(solution)/shard_map/all_gather | solution.py:111
  297.5 0.9 select_bitcast_fusion
  (86 shorter events, 7.0 us)
Async XLA Ops:
  0.6 21.7 %copy-start = (f32[1,8,128,128]{3,2,1,0:T(8,128)S(1)}, f32[1,8,128,128]{3,2,1,0:T(8,128)}, u32[]{:S(2)}) copy-start(f32[1,8,128,128]{3,2,1,0:T(8,128)} %param.13) | copy-start | bytes 1572868
  0.6 1.1 copy-start.3
  0.7 1.2 copy-start.2
  1.8 7.5 %collective-permute-start = (f32[3,1024]{1,0:T(4,128)S(1)}, f32[3,1024]{1,0:T(4,128)S(1)}, u32[]{:S(2)}, u32[]{:S(2)}) collective-permute-start(f32[3,1024]{1,0:T(4,128)S(1)} %pad_maximum_fusion.1), channel_id=1, source_target_pairs={{1,0},{2,1},{3,2},{4,3},{5,4},{6,5},{7,6},{8,7},{9,8},{10,9},{11,1... | collective-permute-start | bytes 36872 | tf_op jit(solution)/shard_map/ppermute | solution.py:15
  7.4 0.9 copy-start.11
  9.6 1.6 copy-start.8
  12.5 9.7 %copy-start.10 = (f32[64,1023]{1,0:T(8,128)S(1)}, f32[64,1023]{1,0:T(8,128)}, u32[]{:S(2)}) copy-start(f32[64,1023]{1,0:T(8,128)} %slice.195) | copy-start | bytes 785668
  12.5 9.7 %copy-start.12 = (f32[1,64,1024]{2,1,0:T(8,128)S(1)}, f32[1,64,1024]{2,1,0:T(8,128)}, u32[]{:S(2)}) copy-start(f32[1,64,1024]{2,1,0:T(8,128)} %param.9) | copy-start | bytes 786436
  12.5 19.3 %all-to-all-start = ((f32[16,1,4096]{2,1,0:T(1,128)}), f32[16,1,4096]{2,1,0:T(1,128)}, u32[]{:S(2)}, u32[]{:S(2)}) async-start(f32[16,1,4096]{2,1,0:T(1,128)} %reshape.295), calls=%async_computation | async-start | bytes 524288 | tf_op jit(solution)/shard_map/all_to_all | solution.py:19
  25.5 10.5 %copy-start.13 = (s32[2,2,1024]{2,1,0:T(2,128)S(1)}, s32[2,2,1024]{2,1,0:T(2,128)}, u32[]{:S(2)}) copy-start(s32[2,2,1024]{2,1,0:T(2,128)} %param.15) | copy-start | bytes 49156
  31.8 12.7 %all-to-all-start.1 = ((f32[16,1,4096]{2,1,0:T(1,128)}), f32[16,1,4096]{2,1,0:T(1,128)}, u32[]{:S(2)}, u32[]{:S(2)}) async-start(f32[16,1,4096]{2,1,0:T(1,128)} %reshape.297), calls=%async_computation.1 | async-start | bytes 524288 | tf_op jit(solution)/shard_map/all_to_all | solution.py:19
  39.9 1.3 copy-start.1
  56.1 14.0 %all-to-all-start.2 = ((f32[16,1,4096]{2,1,0:T(1,128)}), f32[16,1,4096]{2,1,0:T(1,128)S(1)}, u32[]{:S(2)}, u32[]{:S(2)}) async-start(f32[16,1,4096]{2,1,0:T(1,128)} %reshape.299), calls=%async_computation.2 | async-start | bytes 524288 | tf_op jit(solution)/shard_map/all_to_all | solution.py:19
  63.9 0.8 copy-start.4
  73.0 4.7 %collective-permute-start.1 = (f32[1,1024]{1,0:T(1,128)S(1)}, f32[1,1024]{1,0:T(1,128)S(1)}, u32[]{:S(2)}, u32[]{:S(2)}) collective-permute-start(f32[1,1024]{1,0:T(1,128)S(1)} %slice.208), channel_id=1, source_target_pairs={{0,1},{1,2},{2,3},{3,4},{4,5},{5,6},{6,7},{7,8},{8,9},{9,10},{10,1... | collective-permute-start | bytes 12296 | tf_op jit(solution)/shard_map/ppermute | solution.py:15
  163.1 5.6 %collective-permute-start.2 = (f32[3,1024]{1,0:T(4,128)S(1)}, f32[3,1024]{1,0:T(4,128)S(1)}, u32[]{:S(2)}, u32[]{:S(2)}) collective-permute-start(f32[3,1024]{1,0:T(4,128)S(1)} %pad_maximum_fusion), channel_id=1, source_target_pairs={{1,0},{2,1},{3,2},{4,3},{5,4},{6,5},{7,6},{8,7},{9,8},{10,9},{11,1... | collective-permute-start | bytes 36872 | tf_op jit(solution)/shard_map/ppermute | solution.py:15
  164.5 4.2 %copy-start.5 = (f32[8,8,8,128]{3,2,1,0:T(8,128)S(1)}, f32[8,8,8,128]{3,2,1,0:T(8,128)}, u32[]{:S(2)}) copy-start(f32[8,8,8,128]{3,2,1,0:T(8,128)} %copy-done.4) | copy-start | bytes 786436
  169.7 5.8 %copy-start.6 = (f32[64,1024]{1,0:T(8,128)}, f32[64,1024]{1,0:T(8,128)S(1)}, u32[]{:S(2)}) copy-start(f32[64,1024]{1,0:T(8,128)S(1)} %get-tuple-element.12) | copy-start | bytes 786436
  171.9 13.4 %all-to-all-start.3 = ((f32[16,1,4096]{2,1,0:T(1,128)}), f32[16,1,4096]{2,1,0:T(1,128)S(1)}, u32[]{:S(2)}, u32[]{:S(2)}) async-start(f32[16,1,4096]{2,1,0:T(1,128)} %reshape.301), calls=%async_computation.3 | async-start | bytes 524288 | tf_op jit(solution)/shard_map/all_to_all | solution.py:19
  194.9 12.8 %all-to-all-start.4 = ((f32[16,1,4096]{2,1,0:T(1,128)}), f32[16,1,4096]{2,1,0:T(1,128)S(1)}, u32[]{:S(2)}, u32[]{:S(2)}) async-start(f32[16,1,4096]{2,1,0:T(1,128)} %reshape.303), calls=%async_computation.4 | async-start | bytes 524288 | tf_op jit(solution)/shard_map/all_to_all | solution.py:19
  198.4 1.0 copy-start.7
  209.3 2.9 copy-start.9
  209.4 4.7 %collective-permute-start.3 = (f32[1,1024]{1,0:T(1,128)S(1)}, f32[1,1024]{1,0:T(1,128)S(1)}, u32[]{:S(2)}, u32[]{:S(2)}) collective-permute-start(f32[1,1024]{1,0:T(1,128)S(1)} %slice.221), channel_id=1, source_target_pairs={{0,1},{1,2},{2,3},{3,4},{4,5},{5,6},{6,7},{7,8},{8,9},{9,10},{10,1... | collective-permute-start | bytes 12296 | tf_op jit(solution)/shard_map/ppermute | solution.py:15
